TPU v7x, 256 devices: a whole 4x4x8 slice. The times are simulated.
256 devices in a mesh: dp: 2 (over core), row: 16 (over x, y), col: 8 (over z).
Axes of the slice: x: 4, y: 4, z: 8, core: 2. Of those that a mesh axis runs over, the one named last changes fastest.
Arguments:
- tokens: bfloat16 [1536, 8192], P('dp', 'row'), may hold values from -6 to 6
- out_grad: bfloat16 [1536, 8192], P('dp', 'row'), may hold values from -6 to 6
- gate_weight: bfloat16 [8192, 14336], P('row', 'col'), may hold values from -0.0625 to 0.0625
- up_weight: bfloat16 [8192, 14336], P('row', 'col'), may hold values from -0.0625 to 0.0625
- down_weight: bfloat16 [14336, 8192], P('col', 'row'), may hold values from -0.046875 to 0.046875
- gate_mask: int32 [64, 112], P('row', 'col'), may hold values from 0 to 1, as said below
- up_mask: int32 [64, 112], P('row', 'col'), may hold values from 0 to 1, as said below
- down_mask: int32 [112, 64], P('col', 'row'), may hold values from 0 to 1, as said below
Outputs:
- output: bfloat16 [1536, 8192], P(('dp', 'col'), 'row')
- token_grad: bfloat16 [1536, 8192], P(('dp', 'col'), 'row')
- gate_grad: bfloat16 [8192, 14336], P('row', 'col')
- up_grad: bfloat16 [8192, 14336], P('row', 'col')
- down_grad: bfloat16 [14336, 8192], P('col', 'row')
Inputs may be any that keep to these rules, and one draw needn't show every extreme that they name: `gate_mask`: one keep flag for each 128 x 128 block of the matrix; the share kept differs from block row to block row. `up_mask`: one keep flag for each 128 x 128 block of the matrix; the share kept differs from block row to block row. `down_mask`: one keep flag for each 128 x 128 block of the matrix; the share kept differs from block column to block column.
All inputs are finite; a program needn't handle non-finite values.
Results may differ from a plain program's by a relative error of at most 0.029.
Values may be sent and summed in bfloat16 or wider, within the bound.
A program may use at most 128 MiB of HBM per device.

v0:
```python
import jax
import jax.numpy as jnp
from jax import lax
from jax.sharding import PartitionSpec as P

BLOCK = 128


def expand(mask_tile):
    return jnp.repeat(jnp.repeat(mask_tile, BLOCK, axis=0), BLOCK, axis=1)


def contract_rows(left_side, right_side):
    return lax.dot_general(
        left_side, right_side, (((0,), (0,)), ((), ())), preferred_element_type=jnp.float32
    )


def contract_cols(left_side, right_side):
    return lax.dot_general(
        left_side, right_side, (((1,), (1,)), ((), ())), preferred_element_type=jnp.float32
    )


def body(tokens, out_grad, gate_weight, up_weight, down_weight, gate_mask, up_mask, down_mask):
    gate_keep = expand(gate_mask)
    up_keep = expand(up_mask)
    down_keep = expand(down_mask)
    gate_eff = gate_weight * gate_keep.astype(jnp.bfloat16)
    up_eff = up_weight * up_keep.astype(jnp.bfloat16)
    down_eff = down_weight * down_keep.astype(jnp.bfloat16)
    gate_part = jnp.dot(tokens, gate_eff, preferred_element_type=jnp.float32)
    up_part = jnp.dot(tokens, up_eff, preferred_element_type=jnp.float32)
    gate_share, up_share = (
        lax.psum_scatter(
            gate_part.astype(jnp.bfloat16), "row", scatter_dimension=0, tiled=True
        ).astype(jnp.float32),
        lax.psum_scatter(
            up_part.astype(jnp.bfloat16), "row", scatter_dimension=0, tiled=True
        ).astype(jnp.float32),
    )
    gate_sig = jax.nn.sigmoid(gate_share)
    silu_gate = gate_share * gate_sig
    hidden_share = (silu_gate * up_share).astype(jnp.bfloat16)
    hidden = lax.all_gather(hidden_share, "row", axis=0, tiled=True)
    output = lax.psum_scatter(
        jnp.dot(hidden, down_eff, preferred_element_type=jnp.float32).astype(jnp.bfloat16),
        "col",
        scatter_dimension=0,
        tiled=True,
    )
    down_local = contract_rows(hidden, out_grad) * down_keep.astype(jnp.float32)
    back_part = contract_cols(out_grad, down_eff)
    back_share = lax.psum_scatter(
        back_part.astype(jnp.bfloat16), "row", scatter_dimension=0, tiled=True
    ).astype(jnp.float32)
    gate_deriv = (back_share * up_share * gate_sig * (1.0 + gate_share * (1.0 - gate_sig))).astype(
        jnp.bfloat16
    )
    up_deriv = (back_share * silu_gate).astype(jnp.bfloat16)
    gate_full, up_full = (
        lax.all_gather(gate_deriv, "row", axis=0, tiled=True),
        lax.all_gather(up_deriv, "row", axis=0, tiled=True),
    )
    token_grad = lax.psum_scatter(
        (contract_cols(gate_full, gate_eff) + contract_cols(up_full, up_eff)).astype(jnp.bfloat16),
        "col",
        scatter_dimension=0,
        tiled=True,
    )
    gate_local = contract_rows(tokens, gate_full) * gate_keep.astype(jnp.float32)
    up_local = contract_rows(tokens, up_full) * up_keep.astype(jnp.float32)
    gate_total, up_total, down_total = (
        lax.psum(gate_local.astype(jnp.bfloat16), "dp").astype(jnp.float32),
        lax.psum(up_local.astype(jnp.bfloat16), "dp").astype(jnp.float32),
        lax.psum(down_local.astype(jnp.bfloat16), "dp").astype(jnp.float32),
    )
    return (
        output,
        token_grad,
        gate_total.astype(jnp.bfloat16),
        up_total.astype(jnp.bfloat16),
        down_total.astype(jnp.bfloat16),
    )


def solution(mesh):
    placed = (
        P("dp", "row"),
        P("dp", "row"),
        P("row", "col"),
        P("row", "col"),
        P("col", "row"),
        P("row", "col"),
        P("row", "col"),
        P("col", "row"),
    )
    return jax.shard_map(
        body,
        mesh=mesh,
        in_specs=placed,
        out_specs=(
            P(("dp", "col"), "row"),
            P(("dp", "col"), "row"),
            P("row", "col"),
            P("row", "col"),
            P("col", "row"),
        ),
        check_vma=False,
    )
```

profile of v0, /device:TPU:2, one launch (start us, length us, event | category | flops | bytes accessed | tf_op | source)
XLA Modules:
  0.0 568.2 jit_solution(9316289985637627538)
XLA Ops:
  8.2 5.1 broadcast_in_dim.35
  16.2 2.9 copy.59
  19.1 2.8 copy.43
  25.2 2.9 copy.55
  28.2 2.8 copy.46
  34.2 2.9 copy.57
  37.2 66.0 %reduce-scatter.20.cloned.1.call-done = bf16[48,1792]{1,0:T(8,128)(2,1)} async-done(((bf16[768,1792]{1,0:T(8,128)(2,1)}), bf16[48,1792]{1,0:T(8,128)(2,1)}) %reduce-scatter.20.cloned.1.call-update) | async-done | bytes 172048 | tf_op jit(solution)/shard_map/reduce_scatter | solution.py:54
  103.2 84.2 %reduce-scatter.16.cloned.1.call-done = bf16[48,1792]{1,0:T(8,128)(2,1)} async-done(((bf16[768,1792]{1,0:T(8,128)(2,1)}), bf16[48,1792]{1,0:T(8,128)(2,1)}) %reduce-scatter.16.cloned.1.call-update) | async-done | bytes 172048 | tf_op jit(solution)/shard_map/reduce_scatter | solution.py:35
  187.5 84.3 %reduce-scatter.18.cloned.1.call-done = bf16[48,1792]{1,0:T(8,128)(2,1)} async-done(((bf16[768,1792]{1,0:T(8,128)(2,1)}), bf16[48,1792]{1,0:T(8,128)(2,1)}) %reduce-scatter.18.cloned.1.call-update) | async-done | bytes 172048 | tf_op jit(solution)/shard_map/reduce_scatter | solution.py:38
  275.7 48.8 %all-gather.6.cloned.1.call-done = bf16[768,1792]{1,0:T(8,128)(2,1)} async-done(((bf16[48,1792]{1,0:T(8,128)(2,1)}), bf16[768,1792]{1,0:T(8,128)(2,1)}) %all-gather.6.cloned.1.call-update) | async-done | bytes 2752528 | tf_op jit(solution)/shard_map/all_gather | solution.py:62
  324.5 4.7 fusion.2
  329.2 48.4 %all-gather.8.cloned.1.call-done = bf16[768,1792]{1,0:T(8,128)(2,1)} async-done(((bf16[48,1792]{1,0:T(8,128)(2,1)}), bf16[768,1792]{1,0:T(8,128)(2,1)}) %all-gather.8.cloned.1.call-update) | async-done | bytes 2752528 | tf_op jit(solution)/shard_map/all_gather | solution.py:63
  377.6 4.7 fusion.1
  382.3 48.4 %all-gather.4.cloned.1.call-done = bf16[768,1792]{1,0:T(8,128)(2,1)} async-done(((bf16[48,1792]{1,0:T(8,128)(2,1)}), bf16[768,1792]{1,0:T(8,128)(2,1)}) %all-gather.4.cloned.1.call-update) | async-done | bytes 2752528 | tf_op jit(solution)/shard_map/all_gather | solution.py:45
  430.8 2.2 broadcast_in_dim.41
  433.0 2.9 fusion
  436.0 5.5 convolution_convert_fusion.3
  441.6 3.2 fusion.18
  444.8 2.5 add_convert_fusion
  447.3 29.8 %all-reduce.3.cloned.1.call-done = (bf16[512,1792]{0,1:T(8,128)(2,1)}, bf16[512,1792]{0,1:T(8,128)(2,1)}, bf16[1792,512]{1,0:T(8,128)(2,1)}) async-done(((bf16[512,1792]{0,1:T(8,128)(2,1)}, bf16[512,1792]{0,1:T(8,128)(2,1)}, bf16[1792,512]{1,0:T(8,128)(2,1)}), (bf16[512,1792]{0,1:T(8,128)(2,1)}, bf16[512,1792]{0,1:T(8,128)(2,1)}, bf16[1792,512]{1,0:T(8,128)(2,1)})) %all-reduce.3.cloned.1.call-update) | async-done | bytes 5505040 | tf_op jit(solution)/shard_map/psum | solution.py:74
  477.1 3.8 copy.53
  480.9 3.9 copy.54
  484.8 35.0 %reduce-scatter.12.cloned.1.call-done = bf16[96,512]{1,0:T(8,128)(2,1)} async-done(((bf16[768,512]{1,0:T(8,128)(2,1)}), bf16[96,512]{1,0:T(8,128)(2,1)}) %reduce-scatter.12.cloned.1.call-update) | async-done | bytes 98320 | tf_op jit(solution)/shard_map/reduce_scatter | solution.py:46
  519.9 40.1 %reduce-scatter.14.cloned.1.call-done = bf16[96,512]{1,0:T(8,128)(2,1)} async-done(((bf16[768,512]{1,0:T(8,128)(2,1)}), bf16[96,512]{1,0:T(8,128)(2,1)}) %reduce-scatter.14.cloned.1.call-update) | async-done | bytes 98320 | tf_op jit(solution)/shard_map/reduce_scatter | solution.py:65
  (78 shorter events, 16.2 us)
Async XLA Ops:
  7.2 16.4 %copy-start = (bf16[768,512]{1,0:T(8,128)(2,1)S(1)}, bf16[768,512]{1,0:T(8,128)(2,1)}, u32[]{:S(2)}) copy-start(bf16[768,512]{1,0:T(8,128)(2,1)} %param.8) | copy-start | bytes 2359300
  7.2 96.1 %reduce-scatter.20.cloned.1.call-start = ((), (), s32[]{:S(2)}) async-start(), calls=%async_computation.12 | async-start | bytes 2924544 | tf_op jit(solution)/shard_map/reduce_scatter | solution.py:54
  8.1 6.4 %copy-start.12 = (bf16[1792,512]{1,0:T(8,128)(2,1)S(1)}, bf16[1792,512]{1,0:T(8,128)(2,1)}, u32[]{:S(2)}) copy-start(bf16[1792,512]{1,0:T(8,128)(2,1)} %param.12) | copy-start | bytes 5505028
  8.1 6.4 %copy-start.13 = (bf16[768,512]{1,0:T(8,128)(2,1)S(1)}, bf16[768,512]{1,0:T(8,128)(2,1)}, u32[]{:S(2)}) copy-start(bf16[768,512]{1,0:T(8,128)(2,1)} %param.9) | copy-start | bytes 2359300
  13.3 1.2 copy-start.8
  19.1 2.9 copy-start.9
  19.1 168.4 %reduce-scatter.16.cloned.1.call-start = ((), (), s32[]{:S(2)}) async-start(), calls=%async_computation.10 | async-start | bytes 2924544 | tf_op jit(solution)/shard_map/reduce_scatter | solution.py:35
  22.3 1.2 copy-start.4
  28.1 2.9 copy-start.10
  28.1 243.6 %reduce-scatter.18.cloned.1.call-start = ((), (), s32[]{:S(2)}) async-start(), calls=%async_computation.11 | async-start | bytes 2924544 | tf_op jit(solution)/shard_map/reduce_scatter | solution.py:38
  31.4 1.2 copy-start.5
  37.2 287.3 %all-gather.6.cloned.1.call-start = ((), (), s32[]{:S(2)}) async-start(), calls=%async_computation.7 | async-start | bytes 2924544 | tf_op jit(solution)/shard_map/all_gather | solution.py:62
  273.8 103.8 %all-gather.8.cloned.1.call-start = ((), (), s32[]{:S(2)}) async-start(), calls=%async_computation.8 | async-start | bytes 2924544 | tf_op jit(solution)/shard_map/all_gather | solution.py:63
  274.4 156.3 %all-gather.4.cloned.1.call-start = ((), (), s32[]{:S(2)}) async-start(), calls=%async_computation.5 | async-start | bytes 2924544 | tf_op jit(solution)/shard_map/all_gather | solution.py:45
  275.0 202.1 %all-reduce.3.cloned.1.call-start = ((), (), s32[]{:S(2)}) async-start(), calls=%async_computation.13 | async-start | bytes 11010048 | tf_op jit(solution)/shard_map/psum | solution.py:74
  430.7 2.2 copy-start.11
  430.8 2.2 copy-start.14
  435.9 5.7 copy-start.2
  435.9 83.9 %reduce-scatter.12.cloned.1.call-start = ((), (), s32[]{:S(2)}) async-start(), calls=%async_computation.6 | async-start | bytes 884736 | tf_op jit(solution)/shard_map/reduce_scatter | solution.py:46
  441.5 118.5 %reduce-scatter.14.cloned.1.call-start = ((), (), s32[]{:S(2)}) async-start(), calls=%async_computation.9 | async-start | bytes 884736 | tf_op jit(solution)/shard_map/reduce_scatter | solution.py:65
  441.6 3.3 copy-start.3
  441.6 3.3 copy-start.6
  480.9 79.1 %copy-start.7 = (bf16[1792,512]{1,0:T(8,128)(2,1)S(1)}, bf16[1792,512]{1,0:T(8,128)(2,1)}, u32[]{:S(2)}) copy-start(bf16[1792,512]{1,0:T(8,128)(2,1)} %get-tuple-element.41) | copy-start | bytes 5505028
  560.0 1.7 copy-start.1
Sparse Core Ops, SparseCore 0:
  19.2 84.0 reduce-scatter.19
  106.8 80.5 reduce-scatter.15
  191.1 80.5 reduce-scatter.17
  274.1 50.4 all-gather.5
  326.9 50.6 all-gather.7
  379.9 50.6 all-gather.3
  436.0 41.0 all-reduce.2
  480.2 39.6 reduce-scatter.11
  523.0 36.9 reduce-scatter.13
where the time goes:
time: 569 us; the launch traced here: 568 us
  waiting for transfers between devices  486 us (85%)
  local copies, waits for them, and re-layouts  35.8 us (6%)
  matrix products  28.4 us (5%)
  between operations  14.2 us (2%)
    reduce_scatter x1, waiting for transfers between devices, body(): lax.psum_scatter(up_part.astype(jnp.bfloat16), 'row', scatter_dimension=0...  84.3 us
    reduce_scatter x1, waiting for transfers between devices, body(): lax.psum_scatter(gate_part.astype(jnp.bfloat16), 'row', scatter_dimension...  84.2 us
    reduce_scatter x1, waiting for transfers between devices, body(): lax.psum_scatter(back_part.astype(jnp.bfloat16), 'row', scatter_dimension...  66 us
    all_gather x1, waiting for transfers between devices, body(): lax.all_gather(gate_deriv, 'row', axis=0, tiled=True)  48.8 us
    all_gather x1, waiting for transfers between devices, body(): hidden = lax.all_gather(hidden_share, 'row', axis=0, tiled=True)  48.4 us
    all_gather x1, waiting for transfers between devices, body(): lax.all_gather(up_deriv, 'row', axis=0, tiled=True)  48.4 us
    reduce_scatter x1, waiting for transfers between devices, body(): lax.psum_scatter((contract_cols(gate_full, gate_eff) + contract_cols(up_f...  40.1 us
    reduce_scatter x1, waiting for transfers between devices, body(): lax.psum_scatter(jnp.dot(hidden, down_eff, preferred_element_type=jnp.flo...  35 us
  transfers between devices with their start and end apart: 9, of which 9 were waited for; matrix products, arithmetic and copies ran while one was open for 8% of the time, Pallas kernels for 0%

commit v1 on v0

--- a/solution.py
+++ b/solution.py
@@ -4,6 +4,13 @@
 from jax.sharding import PartitionSpec as P
 
 BLOCK = 128
+
+
+def meet_knots(slab_in, dim_k):
+    u_next = list(slab_in.shape[1:])
+    u_next[dim_k] *= slab_in.shape[0]
+    x_next = jnp.moveaxis(slab_in, 0, dim_k).reshape(u_next)
+    return x_next
 
 
 def expand(mask_tile):
@@ -58,8 +65,37 @@
         jnp.bfloat16
     )
     up_deriv = (back_share * silu_gate).astype(jnp.bfloat16)
+
+    def spread_the_patch(here_x, mesh_ax, pos_dim):
+        num = lax.axis_size(mesh_ax)
+        gallery = []
+        for k0 in [*range(num)]:
+            gallery.append((k0, (k0 + 1) % num))
+        so_far_all = []
+        for ii, t in gallery:
+            so_far_all.append((t, ii))
+        found_now, local_out = ([], [])
+        for b in [*range(num - 1)]:
+            if b % 2 == 0:
+                found_now.append(
+                    lax.ppermute(
+                        found_now[-1] if found_now else here_x, axis_name=mesh_ax, perm=gallery
+                    )
+                )
+            else:
+                local_out.append(
+                    lax.ppermute(
+                        local_out[-1] if local_out else here_x, axis_name=mesh_ax, perm=so_far_all
+                    )
+                )
+        block_last = jnp.stack([*found_now[::-1], here_x, *local_out], axis=0)
+        val = lax.axis_index(mesh_ax) - len(found_now)
+        block_last = block_last[(jnp.arange(num) - val) % num]
+        known = meet_knots(block_last, pos_dim)
+        return known
+
     gate_full, up_full = (
-        lax.all_gather(gate_deriv, "row", axis=0, tiled=True),
+        spread_the_patch(gate_deriv, "row", 0),
         lax.all_gather(up_deriv, "row", axis=0, tiled=True),
     )
     token_grad = lax.psum_scatter(

time: 569 us -> 532 us (0.935)
  waiting for transfers between devices: 486 us -> 402 us
  starting transfers between devices: 0.55 us -> 32.6 us
  local copies, waits for them, and re-layouts: 35.8 us -> 50.7 us
    all_gather x1 -> x0, waiting for transfers between devices: 48.8 us -> none  [body(): lax.all_gather(gate_deriv, 'row', axis=0, tiled=True)]
    all_gather x1, waiting for transfers between devices: 48.4 us -> 0.01 us  [body(): lax.all_gather(up_deriv, 'row', axis=0, tiled=True)]
    ppermute x0 -> x15, waiting for transfers between devices: none -> 34.6 us  [the longest x8 20.7 us: spread_the_patch(): lax.ppermute(found_now[-1] if found_now else here_x, axis_name=mesh_ax, p...]
    ppermute x0 -> x15, starting transfers between devices: none -> 32.1 us  [the longest x7 31.7 us: spread_the_patch(): lax.ppermute(local_out[-1] if local_out else here_x, axis_name=mesh_ax, p...]
    reduce_scatter x1, waiting for transfers between devices: 84.3 us -> 61.6 us  [body(): lax.psum_scatter(up_part.astype(jnp.bfloat16), 'row', scatter_dimension=0...]
    reduce_scatter x1, waiting for transfers between devices: 66 us -> 84.4 us  [body(): lax.psum_scatter(back_part.astype(jnp.bfloat16), 'row', scatter_dimension...]
    all_gather x1, waiting for transfers between devices: 48.4 us -> 32.9 us  [body(): hidden = lax.all_gather(hidden_share, 'row', axis=0, tiled=True)]
    unnamed x50 -> x59, local copies, waits for them, and re-layouts: 27.8 us -> 39.5 us
  transfers between devices with their start and end apart: 9 -> 23, of which waited for: 9 -> 21; matrix products, arithmetic and copies ran while one was open for 8% -> 12% of each run, Pallas kernels for 0% -> 0%
where the time goes in v1:
time: 532 us
  waiting for transfers between devices  402 us (76%)
  local copies, waits for them, and re-layouts  50.7 us (10%)
  starting transfers between devices  32.6 us (6%)
  matrix products  29.6 us (6%)
  between operations  14.4 us (3%)
    reduce_scatter x1, waiting for transfers between devices, body(): lax.psum_scatter(back_part.astype(jnp.bfloat16), 'row', scatter_dimension...  84.4 us
    reduce_scatter x1, waiting for transfers between devices, body(): lax.psum_scatter(gate_part.astype(jnp.bfloat16), 'row', scatter_dimension...  84.3 us
    reduce_scatter x1, waiting for transfers between devices, body(): lax.psum_scatter(up_part.astype(jnp.bfloat16), 'row', scatter_dimension=0...  61.6 us
    reduce_scatter x1, waiting for transfers between devices, body(): lax.psum_scatter((contract_cols(gate_full, gate_eff) + contract_cols(up_f...  40.1 us
    unnamed x59, local copies, waits for them, and re-layouts  39.5 us
    reduce_scatter x1, waiting for transfers between devices, body(): lax.psum_scatter(jnp.dot(hidden, down_eff, preferred_element_type=jnp.flo...  35 us
    all_gather x1, waiting for transfers between devices, body(): hidden = lax.all_gather(hidden_share, 'row', axis=0, tiled=True)  32.9 us
    ppermute x7, starting transfers between devices, spread_the_patch(): lax.ppermute(local_out[-1] if local_out else here_x, axis_name=mesh_ax, p...  31.7 us
  transfers between devices with their start and end apart: 23, of which 21 were waited for; matrix products, arithmetic and copies ran while one was open for 12% of the time, Pallas kernels for 0%

profile of v1, /device:TPU:2, one launch (start us, length us, event | category | flops | bytes accessed | tf_op | source)
XLA Modules:
  0.0 531.7 jit_solution(1066148027916991696)
XLA Ops:
  17.1 5.1 broadcast_in_dim.36
  38.8 61.6 %reduce-scatter.18.cloned.1.call-done = bf16[48,1792]{1,0:T(8,128)(2,1)} async-done(((bf16[768,1792]{1,0:T(8,128)(2,1)}), bf16[48,1792]{1,0:T(8,128)(2,1)}) %reduce-scatter.18.cloned.1.call-update) | async-done | bytes 172048 | tf_op jit(solution)/shard_map/reduce_scatter | solution.py:45
  100.5 84.4 %reduce-scatter.20.cloned.1.call-done = bf16[48,1792]{1,0:T(8,128)(2,1)} async-done(((bf16[768,1792]{1,0:T(8,128)(2,1)}), bf16[48,1792]{1,0:T(8,128)(2,1)}) %reduce-scatter.20.cloned.1.call-update) | async-done | bytes 172048 | tf_op jit(solution)/shard_map/reduce_scatter | solution.py:61
  184.9 84.3 %reduce-scatter.16.cloned.1.call-done = bf16[48,1792]{1,0:T(8,128)(2,1)} async-done(((bf16[768,1792]{1,0:T(8,128)(2,1)}), bf16[48,1792]{1,0:T(8,128)(2,1)}) %reduce-scatter.16.cloned.1.call-update) | async-done | bytes 172048 | tf_op jit(solution)/shard_map/reduce_scatter | solution.py:42
  271.6 7.3 %collective-permute-done = bf16[48,1792]{1,0:T(8,128)(2,1)S(1)} collective-permute-done((bf16[48,1792]{1,0:T(8,128)(2,1)S(1)}, bf16[48,1792]{1,0:T(8,128)(2,1)S(1)}, u32[]{:S(2)}, u32[]{:S(2)}) %collective-permute-start) | collective-permute-done | bytes 172064 | tf_op jit(solution)/shard_map/ppermute | solution.py:81
  278.9 4.1 collective-permute-start.8
  283.0 3.4 collective-permute-done.1
  288.0 4.6 collective-permute-start.9
  297.5 4.6 collective-permute-start.10
  306.0 4.6 collective-permute-start.11
  314.8 3.6 collective-permute-done.11
  318.4 4.6 collective-permute-start.12
  327.6 4.6 collective-permute-start.13
  335.1 4.6 collective-permute-start.14
  353.2 3.6 fusion.2
  356.9 4.6 fusion.1
  361.5 32.9 %all-gather.3.cloned.1.call-done = bf16[768,1792]{1,0:T(8,128)(2,1)} async-done(((bf16[48,1792]{1,0:T(8,128)(2,1)}), bf16[768,1792]{1,0:T(8,128)(2,1)}) %all-gather.3.cloned.1.call-update) | async-done | bytes 2752528 | tf_op jit(solution)/shard_map/all_gather | solution.py:52
  399.9 5.4 %convolution_convert_fusion.3 = bf16[768,512]{1,0:T(8,128)(2,1)} fusion(bf16[768,1792]{1,0:T(8,128)(2,1)} %all-gather.3.cloned.1.call-done, bf16[1792,512]{1,0:T(8,128)(2,1)} %param.12, bf16[224,8,4,128]{3,2,1,0:T(4,128)(2,1)} %bitcast.117), kind=kOutput, calls=%fused_computation.17 | convolution fusion | flops 1410596864 | bytes 7208960 | tf_op jit(solution)/shard_map/dot_general | solution.py:54
  405.3 4.0 fusion.20
  411.8 28.9 %all-reduce.3.cloned.1.call-done = (bf16[512,1792]{0,1:T(8,128)(2,1)}, bf16[512,1792]{0,1:T(8,128)(2,1)}, bf16[1792,512]{1,0:T(8,128)(2,1)}) async-done(((bf16[512,1792]{0,1:T(8,128)(2,1)}, bf16[512,1792]{0,1:T(8,128)(2,1)}, bf16[1792,512]{1,0:T(8,128)(2,1)}), (bf16[512,1792]{0,1:T(8,128)(2,1)}, bf16[512,1792]{0,1:T(8,128)(2,1)}, bf16[1792,512]{1,0:T(8,128)(2,1)})) %all-reduce.3.cloned.1.call-update) | async-done | bytes 5505040 | tf_op jit(solution)/shard_map/psum | solution.py:110
  440.8 3.8 copy.69
  444.6 3.9 copy.70
  448.5 35.0 %reduce-scatter.12.cloned.1.call-done = bf16[96,512]{1,0:T(8,128)(2,1)} async-done(((bf16[768,512]{1,0:T(8,128)(2,1)}), bf16[96,512]{1,0:T(8,128)(2,1)}) %reduce-scatter.12.cloned.1.call-update) | async-done | bytes 98320 | tf_op jit(solution)/shard_map/reduce_scatter | solution.py:53
  483.5 40.1 %reduce-scatter.14.cloned.1.call-done = bf16[96,512]{1,0:T(8,128)(2,1)} async-done(((bf16[768,512]{1,0:T(8,128)(2,1)}), bf16[96,512]{1,0:T(8,128)(2,1)}) %reduce-scatter.14.cloned.1.call-update) | async-done | bytes 98320 | tf_op jit(solution)/shard_map/reduce_scatter | solution.py:101
  (118 shorter events, 73.5 us)
Async XLA Ops:
  7.2 93.3 %reduce-scatter.18.cloned.1.call-start = ((), (), s32[]{:S(2)}) async-start(), calls=%async_computation.10 | async-start | bytes 2924544 | tf_op jit(solution)/shard_map/reduce_scatter | solution.py:45
  16.2 168.6 %reduce-scatter.20.cloned.1.call-start = ((), (), s32[]{:S(2)}) async-start(), calls=%async_computation.11 | async-start | bytes 2924544 | tf_op jit(solution)/shard_map/reduce_scatter | solution.py:61
  29.7 239.4 %reduce-scatter.16.cloned.1.call-start = ((), (), s32[]{:S(2)}) async-start(), calls=%async_computation.9 | async-start | bytes 2924544 | tf_op jit(solution)/shard_map/reduce_scatter | solution.py:42
  38.8 318.1 %all-gather.5.cloned.1.call-start = ((), (), s32[]{:S(2)}) async-start(), calls=%async_computation.7 | async-start | bytes 2924544 | tf_op jit(solution)/shard_map/all_gather | solution.py:99
  271.2 123.1 %all-gather.3.cloned.1.call-start = ((), (), s32[]{:S(2)}) async-start(), calls=%async_computation.5 | async-start | bytes 2924544 | tf_op jit(solution)/shard_map/all_gather | solution.py:52
  271.3 7.6 %collective-permute-start = (bf16[48,1792]{1,0:T(8,128)(2,1)S(1)}, bf16[48,1792]{1,0:T(8,128)(2,1)S(1)}, u32[]{:S(2)}, u32[]{:S(2)}) collective-permute-start(bf16[48,1792]{1,0:T(8,128)(2,1)S(1)} %get-tuple-element.28), channel_id=1, source_target_pairs={{0,8},{8,16},{16,24},{24,32},{32,40},{40,48},{48,56},{56,64},{64,7... | collective-permute-start | bytes 516104 | tf_op jit(solution)/shard_map/ppermute | solution.py:81
  278.9 7.5 %collective-permute-start.1 = (bf16[48,1792]{1,0:T(8,128)(2,1)S(1)}, bf16[48,1792]{1,0:T(8,128)(2,1)S(1)}, u32[]{:S(2)}, u32[]{:S(2)}) collective-permute-start(bf16[48,1792]{1,0:T(8,128)(2,1)S(1)} %collective-permute-done), channel_id=1, source_target_pairs={{0,8},{8,16},{16,24},{24,32},{32,40},{40,48},{48,56},{56,64},{64,7... | collective-permute-start | bytes 516104 | tf_op jit(solution)/shard_map/ppermute | solution.py:81
  278.9 9.1 %collective-permute-start.8 = (bf16[48,1792]{1,0:T(8,128)(2,1)S(1)}, bf16[48,1792]{1,0:T(8,128)(2,1)S(1)}, u32[]{:S(2)}, u32[]{:S(2)}) collective-permute-start(bf16[48,1792]{1,0:T(8,128)(2,1)S(1)} %get-tuple-element.28), channel_id=1, source_target_pairs={{8,0},{16,8},{24,16},{32,24},{40,32},{48,40},{56,48},{64,56},{72,6... | collective-permute-start | bytes 516104 | tf_op jit(solution)/shard_map/ppermute | solution.py:87
  286.4 9.0 %collective-permute-start.2 = (bf16[48,1792]{1,0:T(8,128)(2,1)S(1)}, bf16[48,1792]{1,0:T(8,128)(2,1)S(1)}, u32[]{:S(2)}, u32[]{:S(2)}) collective-permute-start(bf16[48,1792]{1,0:T(8,128)(2,1)S(1)} %collective-permute-done.1), channel_id=1, source_target_pairs={{0,8},{8,16},{16,24},{24,32},{32,40},{40,48},{48,56},{56,64},{64,7... | collective-permute-start | bytes 516104 | tf_op jit(solution)/shard_map/ppermute | solution.py:81
  288.0 9.5 %collective-permute-start.9 = (bf16[48,1792]{1,0:T(8,128)(2,1)S(1)}, bf16[48,1792]{1,0:T(8,128)(2,1)S(1)}, u32[]{:S(2)}, u32[]{:S(2)}) collective-permute-start(bf16[48,1792]{1,0:T(8,128)(2,1)S(1)} %collective-permute-done.8), channel_id=1, source_target_pairs={{8,0},{16,8},{24,16},{32,24},{40,32},{48,40},{56,48},{64,56},{72,6... | collective-permute-start | bytes 516104 | tf_op jit(solution)/shard_map/ppermute | solution.py:87
  295.4 8.6 %collective-permute-start.3 = (bf16[48,1792]{1,0:T(8,128)(2,1)S(1)}, bf16[48,1792]{1,0:T(8,128)(2,1)S(1)}, u32[]{:S(2)}, u32[]{:S(2)}) collective-permute-start(bf16[48,1792]{1,0:T(8,128)(2,1)S(1)} %collective-permute-done.2), channel_id=1, source_target_pairs={{0,8},{8,16},{16,24},{24,32},{32,40},{40,48},{48,56},{56,64},{64,7... | collective-permute-start | bytes 516104 | tf_op jit(solution)/shard_map/ppermute | solution.py:81
  297.5 8.5 %collective-permute-start.10 = (bf16[48,1792]{1,0:T(8,128)(2,1)S(1)}, bf16[48,1792]{1,0:T(8,128)(2,1)S(1)}, u32[]{:S(2)}, u32[]{:S(2)}) collective-permute-start(bf16[48,1792]{1,0:T(8,128)(2,1)S(1)} %collective-permute-done.9), channel_id=1, source_target_pairs={{8,0},{16,8},{24,16},{32,24},{40,32},{48,40},{56,48},{64,56},{72,6... | collective-permute-start | bytes 516104 | tf_op jit(solution)/shard_map/ppermute | solution.py:87
  304.0 10.0 %collective-permute-start.4 = (bf16[48,1792]{1,0:T(8,128)(2,1)S(1)}, bf16[48,1792]{1,0:T(8,128)(2,1)S(1)}, u32[]{:S(2)}, u32[]{:S(2)}) collective-permute-start(bf16[48,1792]{1,0:T(8,128)(2,1)S(1)} %collective-permute-done.3), channel_id=1, source_target_pairs={{0,8},{8,16},{16,24},{24,32},{32,40},{40,48},{48,56},{56,64},{64,7... | collective-permute-start | bytes 516104 | tf_op jit(solution)/shard_map/ppermute | solution.py:81
  306.0 12.4 %collective-permute-start.11 = (bf16[48,1792]{1,0:T(8,128)(2,1)S(1)}, bf16[48,1792]{1,0:T(8,128)(2,1)S(1)}, u32[]{:S(2)}, u32[]{:S(2)}) collective-permute-start(bf16[48,1792]{1,0:T(8,128)(2,1)S(1)} %collective-permute-done.10), channel_id=1, source_target_pairs={{8,0},{16,8},{24,16},{32,24},{40,32},{48,40},{56,48},{64,56},{72,6... | collective-permute-start | bytes 516104 | tf_op jit(solution)/shard_map/ppermute | solution.py:87
  313.9 10.8 %collective-permute-start.5 = (bf16[48,1792]{1,0:T(8,128)(2,1)S(1)}, bf16[48,1792]{1,0:T(8,128)(2,1)S(1)}, u32[]{:S(2)}, u32[]{:S(2)}) collective-permute-start(bf16[48,1792]{1,0:T(8,128)(2,1)S(1)} %collective-permute-done.4), channel_id=1, source_target_pairs={{0,8},{8,16},{16,24},{24,32},{32,40},{40,48},{48,56},{56,64},{64,7... | collective-permute-start | bytes 516104 | tf_op jit(solution)/shard_map/ppermute | solution.py:81
  318.4 9.2 %collective-permute-start.12 = (bf16[48,1792]{1,0:T(8,128)(2,1)S(1)}, bf16[48,1792]{1,0:T(8,128)(2,1)S(1)}, u32[]{:S(2)}, u32[]{:S(2)}) collective-permute-start(bf16[48,1792]{1,0:T(8,128)(2,1)S(1)} %collective-permute-done.11), channel_id=1, source_target_pairs={{8,0},{16,8},{24,16},{32,24},{40,32},{48,40},{56,48},{64,56},{72,6... | collective-permute-start | bytes 516104 | tf_op jit(solution)/shard_map/ppermute | solution.py:87
  324.7 7.6 %collective-permute-start.6 = (bf16[48,1792]{1,0:T(8,128)(2,1)S(1)}, bf16[48,1792]{1,0:T(8,128)(2,1)S(1)}, u32[]{:S(2)}, u32[]{:S(2)}) collective-permute-start(bf16[48,1792]{1,0:T(8,128)(2,1)S(1)} %collective-permute-done.5), channel_id=1, source_target_pairs={{0,8},{8,16},{16,24},{24,32},{32,40},{40,48},{48,56},{56,64},{64,7... | collective-permute-start | bytes 516104 | tf_op jit(solution)/shard_map/ppermute | solution.py:81
  327.6 7.5 %collective-permute-start.13 = (bf16[48,1792]{1,0:T(8,128)(2,1)S(1)}, bf16[48,1792]{1,0:T(8,128)(2,1)S(1)}, u32[]{:S(2)}, u32[]{:S(2)}) collective-permute-start(bf16[48,1792]{1,0:T(8,128)(2,1)S(1)} %collective-permute-done.12), channel_id=1, source_target_pairs={{8,0},{16,8},{24,16},{32,24},{40,32},{48,40},{56,48},{64,56},{72,6... | collective-permute-start | bytes 516104 | tf_op jit(solution)/shard_map/ppermute | solution.py:87
  332.3 7.5 %collective-permute-start.7 = (bf16[48,1792]{1,0:T(8,128)(2,1)S(1)}, bf16[48,1792]{1,0:T(8,128)(2,1)S(1)}, u32[]{:S(2)}, u32[]{:S(2)}) collective-permute-start(bf16[48,1792]{1,0:T(8,128)(2,1)S(1)} %collective-permute-done.6), channel_id=1, source_target_pairs={{0,8},{8,16},{16,24},{24,32},{32,40},{40,48},{48,56},{56,64},{64,7... | collective-permute-start | bytes 516104 | tf_op jit(solution)/shard_map/ppermute | solution.py:81
  332.4 108.4 %all-reduce.3.cloned.1.call-start = ((), (), s32[]{:S(2)}) async-start(), calls=%async_computation.12 | async-start | bytes 11010048 | tf_op jit(solution)/shard_map/psum | solution.py:110
  335.1 15.0 %collective-permute-start.14 = (bf16[48,1792]{1,0:T(8,128)(2,1)S(1)}, bf16[48,1792]{1,0:T(8,128)(2,1)S(1)}, u32[]{:S(2)}, u32[]{:S(2)}) collective-permute-start(bf16[48,1792]{1,0:T(8,128)(2,1)S(1)} %collective-permute-done.13), channel_id=1, source_target_pairs={{8,0},{16,8},{24,16},{32,24},{40,32},{48,40},{56,48},{64,56},{72,6... | collective-permute-start | bytes 516104 | tf_op jit(solution)/shard_map/ppermute | solution.py:87
  399.6 83.9 %reduce-scatter.12.cloned.1.call-start = ((), (), s32[]{:S(2)}) async-start(), calls=%async_computation.6 | async-start | bytes 884736 | tf_op jit(solution)/shard_map/reduce_scatter | solution.py:53
  405.2 118.4 %reduce-scatter.14.cloned.1.call-start = ((), (), s32[]{:S(2)}) async-start(), calls=%async_computation.8 | async-start | bytes 884736 | tf_op jit(solution)/shard_map/reduce_scatter | solution.py:101
  444.6 80.3 %copy-start.1 = (bf16[768,512]{1,0:T(8,128)(2,1)S(1)}, bf16[768,512]{1,0:T(8,128)(2,1)}, u32[]{:S(2)}) copy-start(bf16[768,512]{1,0:T(8,128)(2,1)} %param.8) | copy-start | bytes 2359300
  (11 other events, 135.4 us)
Sparse Core Ops, SparseCore 0:
  16.4 84.0 reduce-scatter.17
  104.1 80.7 reduce-scatter.19
  188.5 80.6 reduce-scatter.15
  271.5 57.1 all-gather.4
  332.5 61.8 all-gather.2
  399.7 41.0 all-reduce.2
  443.9 39.6 reduce-scatter.11
  486.6 36.9 reduce-scatter.13
